TPU v7x, 32 devices: a whole 2x2x4 slice. The times are simulated.
32 devices in a mesh: dp: 16 (over z, y, x), mp: 2 (over core).
Axes of the slice: x: 2, y: 2, z: 4, core: 2. Of those that a mesh axis runs over, the one named last changes fastest.
Arguments:
- inputs: bfloat16 [16, 1024, 768], P('dp'), may hold values from -6 to 6
- segments: int32 [16, 1024], P('dp'), may hold values from 0 to 28, as said below
- cotangent: bfloat16 [16, 1024, 768], P('dp'), may hold values from -6 to 6
- norm1_gain: float32 [768], replicated, may hold values from 0.5 to 1.5
- norm1_bias: float32 [768], replicated, may hold values from -3 to 3
- qkv_weight: bfloat16 [3, 768, 768], P(None, None, 'mp'), may hold values from -0.21875 to 0.21875
- qv_bias: float32 [2, 768], P(None, 'mp'), may hold values from -3 to 3
- proj_weight: bfloat16 [768, 768], P('mp'), may hold values from -1.75 to 1.75
- proj_bias: float32 [768], replicated, may hold values from -3 to 3
- norm2_gain: float32 [768], replicated, may hold values from 0.5 to 1.5
- norm2_bias: float32 [768], replicated, may hold values from -3 to 3
- fc1_weight: bfloat16 [768, 3072], P(None, 'mp'), may hold values from -0.21875 to 0.21875
- fc1_bias: float32 [3072], P('mp'), may hold values from -3 to 3
- fc2_weight: bfloat16 [3072, 768], P('mp'), may hold values from -0.109375 to 0.109375
- fc2_bias: float32 [768], replicated, may hold values from -3 to 3
Outputs:
- output: bfloat16 [16, 1024, 768], P('dp')
- input_grad: bfloat16 [16, 1024, 768], P('dp')
- norm1_gain_grad: float32 [768], P('dp')
- norm1_bias_grad: float32 [768], P('dp')
- qkv_weight_grad: float32 [3, 768, 768], P(None, 'dp', 'mp')
- qv_bias_grad: float32 [2, 768], P(None, ('mp', 'dp'))
- proj_weight_grad: float32 [768, 768], P('mp', 'dp')
- proj_bias_grad: float32 [768], P('dp')
- norm2_gain_grad: float32 [768], P('dp')
- norm2_bias_grad: float32 [768], P('dp')
- fc1_weight_grad: float32 [768, 3072], P('dp', 'mp')
- fc1_bias_grad: float32 [3072], P(('mp', 'dp'))
- fc2_weight_grad: float32 [3072, 768], P('mp', 'dp')
- fc2_bias_grad: float32 [768], P('dp')
Inputs may be any that keep to these rules, and one draw needn't show every extreme that they name: `segments`: each packed row holds whole images from slot 0 onward, numbered 1, 2, 3 and so on in order, each a run of max(1024 * n // 1024, 1) slots for n one of 576, 400, 256, 225, 144, 100, 64, 36 (patch-size classes of a 240-pixel image); the slots after the last image are 0. One packed row holds only images of the smallest class, as many as fit.
All inputs are finite; a program needn't handle non-finite values.
Results may differ from a plain program's by a relative error of at most 0.013.
Values sent between devices are 32-bit elements; how exact they have to be, the bound alone decides.
No kernel may reach another device: no remote copies, remote signals or barrier semaphores. Data moves between devices by JAX's collectives and lax.ppermute only.
A program may use at most 192 MiB of HBM per device.

v0:
```python
from functools import partial
import jax
import jax.numpy as jnp
from jax import lax
from jax.sharding import PartitionSpec as P

HEAD_DIM = 64
EPSILON = 1e-06
NEG_FILL = -1000000000.0


def layer_norm(values, gain_vec, shift_vec):
    center = values - jnp.mean(values, axis=-1, keepdims=True)
    inv_spread = lax.rsqrt(jnp.mean(center * center, axis=-1, keepdims=True) + EPSILON)
    normed = center * inv_spread
    return (normed * gain_vec + shift_vec, normed, inv_spread)


def norm_back(grad_out, normed, inv_spread, gain_vec):
    scaled = grad_out * gain_vec
    grad_in = inv_spread * (
        scaled
        - jnp.mean(scaled, axis=-1, keepdims=True)
        - normed * jnp.mean(scaled * normed, axis=-1, keepdims=True)
    )
    return (grad_in, jnp.sum(grad_out * normed, axis=0), jnp.sum(grad_out, axis=0))


def product(left_side, right_side):
    return jnp.dot(left_side, right_side, preferred_element_type=jnp.float32)


def row_contract(left_side, right_side):
    return lax.dot_general(
        left_side, right_side, (((0,), (0,)), ((), ())), preferred_element_type=jnp.float32
    )


def back_product(left_side, right_side):
    return lax.dot_general(
        left_side, right_side, (((1,), (1,)), ((), ())), preferred_element_type=jnp.float32
    )


def block_scores(query_block, key_heads, seg_block, seg_row, score_scale):
    scores = (
        jnp.einsum("qhd,khd->hqk", query_block, key_heads, preferred_element_type=jnp.float32)
        * score_scale
    )
    allowed = (seg_block[:, None] == seg_row[None, :]) & (seg_block[:, None] > 0)
    return jnp.where(allowed[None], scores, NEG_FILL)


def row_forward(operands):
    query_row, key_row, value_row, seg_row = operands
    seq_len = query_row.shape[0]
    head_count = query_row.shape[1] // HEAD_DIM
    block_len = min(512, seq_len)
    score_scale = HEAD_DIM ** (-0.5)
    query_heads = query_row.reshape(seq_len, head_count, HEAD_DIM)
    key_heads = key_row.reshape(seq_len, head_count, HEAD_DIM)
    value_heads = value_row.reshape(seq_len, head_count, HEAD_DIM)
    outputs = []
    log_parts = []
    for offset in range(0, seq_len, block_len):
        scores = block_scores(
            query_heads[offset : offset + block_len],
            key_heads,
            seg_row[offset : offset + block_len],
            seg_row,
            score_scale,
        )
        row_max = jnp.max(scores, axis=-1, keepdims=True)
        exponent = jnp.exp(scores - row_max)
        row_total = jnp.sum(exponent, axis=-1, keepdims=True)
        weights = (exponent / row_total).astype(jnp.bfloat16)
        mixed_rows = jnp.einsum(
            "hqk,khd->qhd", weights, value_heads, preferred_element_type=jnp.float32
        )
        outputs.append(mixed_rows.reshape(block_len, head_count * HEAD_DIM))
        log_parts.append((row_max + jnp.log(row_total))[..., 0])
    return (jnp.concatenate(outputs, axis=0), jnp.concatenate(log_parts, axis=1))


def row_backward(operands):
    query_row, key_row, value_row, seg_row, grad_row, log_total = operands
    seq_len = query_row.shape[0]
    head_count = query_row.shape[1] // HEAD_DIM
    block_len = min(512, seq_len)
    score_scale = HEAD_DIM ** (-0.5)
    query_heads = query_row.reshape(seq_len, head_count, HEAD_DIM)
    key_heads = key_row.reshape(seq_len, head_count, HEAD_DIM)
    value_heads = value_row.reshape(seq_len, head_count, HEAD_DIM)
    grad_heads = grad_row.reshape(seq_len, head_count, HEAD_DIM)
    key_grad = jnp.zeros((seq_len, head_count, HEAD_DIM), jnp.float32)
    value_grad = jnp.zeros((seq_len, head_count, HEAD_DIM), jnp.float32)
    query_parts = []
    for offset in range(0, seq_len, block_len):
        query_block = query_heads[offset : offset + block_len]
        grad_block = grad_heads[offset : offset + block_len]
        scores = block_scores(
            query_block, key_heads, seg_row[offset : offset + block_len], seg_row, score_scale
        )
        weights = jnp.exp(scores - log_total[:, offset : offset + block_len, None])
        weights_low = weights.astype(jnp.bfloat16)
        grad_weights = jnp.einsum(
            "qhd,khd->hqk", grad_block, value_heads, preferred_element_type=jnp.float32
        )
        grad_scores = (
            weights * (grad_weights - jnp.sum(weights * grad_weights, axis=-1, keepdims=True))
        ).astype(jnp.bfloat16)
        query_parts.append(
            (
                jnp.einsum(
                    "hqk,khd->qhd", grad_scores, key_heads, preferred_element_type=jnp.float32
                )
                * score_scale
            ).reshape(block_len, head_count * HEAD_DIM)
        )
        key_grad = (
            key_grad
            + jnp.einsum(
                "hqk,qhd->khd", grad_scores, query_block, preferred_element_type=jnp.float32
            )
            * score_scale
        )
        value_grad = value_grad + jnp.einsum(
            "hqk,qhd->khd", weights_low, grad_block, preferred_element_type=jnp.float32
        )
    query_grad = jnp.concatenate(query_parts, axis=0).astype(jnp.bfloat16)
    flat_width = head_count * HEAD_DIM
    return (
        query_grad,
        key_grad.reshape(seq_len, flat_width).astype(jnp.bfloat16),
        value_grad.reshape(seq_len, flat_width).astype(jnp.bfloat16),
    )


def shards(
    inputs,
    segments,
    cotangent,
    norm1_gain,
    norm1_bias,
    qkv_weight,
    qv_bias,
    proj_weight,
    proj_bias,
    norm2_gain,
    norm2_bias,
    fc1_weight,
    fc1_bias,
    fc2_weight,
    fc2_bias,
):
    pack_count, seq_len, model_width = inputs.shape
    row_count = pack_count * seq_len
    local_width = qkv_weight.shape[2]
    row_shape = (pack_count, seq_len, local_width)
    live_rows = (segments > 0).astype(jnp.float32).reshape(row_count, 1)
    flat_in = inputs.reshape(row_count, model_width).astype(jnp.float32)
    norm1_out, norm1_hat, norm1_inv = layer_norm(flat_in, norm1_gain, norm1_bias)
    norm1_low = norm1_out.astype(jnp.bfloat16)
    queries = (product(norm1_low, qkv_weight[0]) + qv_bias[0]).astype(jnp.bfloat16)
    key_rows = product(norm1_low, qkv_weight[1]).astype(jnp.bfloat16)
    value_rows = (product(norm1_low, qkv_weight[2]) + qv_bias[1]).astype(jnp.bfloat16)
    query_packs = queries.reshape(row_shape)
    key_packs = key_rows.reshape(row_shape)
    value_packs = value_rows.reshape(row_shape)
    mixed_rows, log_total = lax.map(row_forward, (query_packs, key_packs, value_packs, segments))
    attended = (mixed_rows.reshape(row_count, local_width) * live_rows).astype(jnp.bfloat16)
    branch = lax.psum(product(attended, proj_weight), "mp") + proj_bias
    middle = flat_in + branch
    norm2_out, norm2_hat, norm2_inv = layer_norm(middle, norm2_gain, norm2_bias)
    norm2_low = norm2_out.astype(jnp.bfloat16)
    hidden = product(norm2_low, fc1_weight) + fc1_bias
    active, gelu_pull = jax.vjp(partial(jax.nn.gelu, approximate=False), hidden)
    active_low = active.astype(jnp.bfloat16)
    result = middle + (lax.psum(product(active_low, fc2_weight), "mp") + fc2_bias)
    output = result.astype(jnp.bfloat16).reshape(pack_count, seq_len, model_width)
    grad_top = cotangent.reshape(row_count, model_width).astype(jnp.float32) * live_rows
    grad_top_low = grad_top.astype(jnp.bfloat16)
    fc2_grad = row_contract(active_low, grad_top_low)
    fc2_bias_grad = jnp.sum(grad_top, axis=0)
    grad_active = back_product(grad_top_low, fc2_weight)
    grad_hidden = gelu_pull(grad_active)[0].astype(jnp.bfloat16)
    fc1_grad = row_contract(norm2_low, grad_hidden)
    fc1_bias_grad = jnp.sum(grad_hidden, axis=0, dtype=jnp.float32)
    grad_norm2 = lax.psum(back_product(grad_hidden, fc1_weight), "mp")
    grad_mid_norm, norm2_gain_grad, norm2_bias_grad = norm_back(
        grad_norm2, norm2_hat, norm2_inv, norm2_gain
    )
    grad_middle = grad_top + grad_mid_norm
    grad_branch = grad_middle.astype(jnp.bfloat16)
    proj_grad = row_contract(attended, grad_branch)
    proj_bias_grad = jnp.sum(grad_branch, axis=0, dtype=jnp.float32)
    grad_attended = back_product(grad_branch, proj_weight).astype(jnp.bfloat16) * live_rows.astype(
        jnp.bfloat16
    )
    query_grad, key_grad, value_grad = lax.map(
        row_backward,
        (
            query_packs,
            key_packs,
            value_packs,
            segments,
            grad_attended.reshape(row_shape),
            log_total,
        ),
    )
    query_grad = query_grad.reshape(row_count, local_width)
    key_grad = key_grad.reshape(row_count, local_width)
    value_grad = value_grad.reshape(row_count, local_width)
    qkv_grad = jnp.stack(
        [
            row_contract(norm1_low, query_grad),
            row_contract(norm1_low, key_grad),
            row_contract(norm1_low, value_grad),
        ]
    )
    qv_bias_grad = jnp.stack(
        [
            jnp.sum(query_grad, axis=0, dtype=jnp.float32),
            jnp.sum(value_grad, axis=0, dtype=jnp.float32),
        ]
    )
    grad_norm1 = lax.psum(
        back_product(query_grad, qkv_weight[0])
        + back_product(key_grad, qkv_weight[1])
        + back_product(value_grad, qkv_weight[2]),
        "mp",
    )
    grad_in_norm, norm1_gain_grad, norm1_bias_grad = norm_back(
        grad_norm1, norm1_hat, norm1_inv, norm1_gain
    )
    input_grad = (
        (grad_middle + grad_in_norm).astype(jnp.bfloat16).reshape(pack_count, seq_len, model_width)
    )
    every_sum = (
        lax.psum_scatter(norm1_gain_grad, "dp", scatter_dimension=0, tiled=True),
        lax.psum_scatter(norm1_bias_grad, "dp", scatter_dimension=0, tiled=True),
        lax.psum_scatter(qkv_grad, "dp", scatter_dimension=1, tiled=True),
        lax.psum_scatter(qv_bias_grad, "dp", scatter_dimension=1, tiled=True),
        lax.psum_scatter(proj_grad, "dp", scatter_dimension=1, tiled=True),
        lax.psum_scatter(proj_bias_grad, "dp", scatter_dimension=0, tiled=True),
        lax.psum_scatter(norm2_gain_grad, "dp", scatter_dimension=0, tiled=True),
        lax.psum_scatter(norm2_bias_grad, "dp", scatter_dimension=0, tiled=True),
        lax.psum_scatter(fc1_grad, "dp", scatter_dimension=0, tiled=True),
        lax.psum_scatter(fc1_bias_grad, "dp", scatter_dimension=0, tiled=True),
        lax.psum_scatter(fc2_grad, "dp", scatter_dimension=1, tiled=True),
        lax.psum_scatter(fc2_bias_grad, "dp", scatter_dimension=0, tiled=True),
    )
    return (
        output,
        input_grad,
        every_sum[0],
        every_sum[1],
        every_sum[2],
        every_sum[3],
        every_sum[4],
        every_sum[5],
        every_sum[6],
        every_sum[7],
        every_sum[8],
        every_sum[9],
        every_sum[10],
        every_sum[11],
    )


def solution(mesh):
    placed = (
        P("dp", None, None),
        P("dp", None),
        P("dp", None, None),
        P(),
        P(),
        P(None, None, "mp"),
        P(None, "mp"),
        P("mp", None),
        P(),
        P(),
        P(),
        P(None, "mp"),
        P("mp"),
        P("mp", None),
        P(),
    )
    return jax.shard_map(
        shards,
        mesh=mesh,
        in_specs=placed,
        out_specs=(
            P("dp", None, None),
            P("dp", None, None),
            P("dp"),
            P("dp"),
            P(None, "dp", "mp"),
            P(None, ("mp", "dp")),
            P("mp", "dp"),
            P("dp"),
            P("dp"),
            P("dp"),
            P("dp", "mp"),
            P(("mp", "dp")),
            P("mp", "dp"),
            P("dp"),
        ),
        check_vma=False,
    )
```

profile of v0, /device:TPU:0, one launch (start us, length us, event | category | flops | bytes accessed | tf_op | source)
XLA Modules:
  0.0 792.5 jit_solution(12064317991579833451)
XLA Ops:
  20.1 2.8 fusion.1
  24.6 3.8 fusion.17
  30.8 2.8 fusion
  35.5 3.8 fusion.16
  43.1 26.1 %all-reduce.14.cloned.1.call-done = f32[1024,768]{1,0:T(8,128)} async-done(((f32[1024,768]{1,0:T(8,128)}), f32[1024,768]{1,0:T(8,128)}) %all-reduce.14.cloned.1.call-update) | async-done | bytes 3145744 | tf_op jit(solution)/shard_map/psum | solution.py:172
  69.2 2.8 fusion.94
  72.9 17.2 %multiply_convert_fusion.2 = (bf16[1024,1536]{1,0:T(8,128)(2,1)}, f32[1024,1536]{1,0:T(8,128)S(1)}, f32[1024,1536]{1,0:T(8,128)S(1)}) fusion(f32[1536]{0:T(1024)S(1)} %copy-done.67, bf16[768,1536]{1,0:T(8,128)(2,1)S(1)} %copy-done, f32[1024,768]{1,0:T(8,128)S(1)} %get-tuple-element.90, f32[768]{0:T(1024)S(1)} %copy-done.68, f32[768]{0:T(1024)S(1)} %copy-done.56, ...), kind=kOutput, calls=%fused_computation.24 | convolution fusion | flops 2523660288 | bytes 21254144 | tf_op jit(solution)/shard_map/dot_general | solution.py:30
  90.1 5.6 convert_reduce_fusion
  97.5 4.3 fusion.102
  103.2 7.0 fusion.101
  110.3 16.2 %all-reduce.16.cloned.1.call-done = f32[1024,768]{1,0:T(8,128)} async-done(((f32[1024,768]{1,0:T(8,128)}), f32[1024,768]{1,0:T(8,128)}) %all-reduce.16.cloned.1.call-update) | async-done | bytes 3145744 | tf_op jit(solution)/shard_map/psum | solution.py:189
  126.5 4.5 multiply_reduce_fusion.2
  131.1 4.3 convert_reduce_fusion.2
  138.8 6.2 multiply_reduce_fusion.1
  145.0 10.0 %multiply_convert_fusion.1 = bf16[6,512,1024]{2,1,0:T(8,128)(2,1)} fusion(f32[6,512,1024]{2,1,0:T(8,128)} %get-tuple-element.108, f32[6,512,1024]{2,1,0:T(8,128)S(1)} %bitcast.153, f32[6,512]{1,0:T(8,128)S(1)} %get-tuple-element.107, f32[6,512]{1,0:T(8,128)S(1)} %log_add_fusion.1), kind=kLoop, calls=%fused_computation.3 | loop fusion | flops 12582912 | bytes 31481856 | tf_op jit(solution)/shard_map/while/body/eval_jaxpr/convert_element_type | solution.py:111
  155.0 5.0 fusion.58
  160.0 4.0 fusion.103
  164.1 3.3 fusion.5
  167.4 7.5 multiply_reduce_fusion
  174.9 5.0 convert_reduce_fusion.3
  179.8 6.6 multiply_convert_fusion
  192.2 2.8 add_add_fusion
  196.1 4.2 fusion.80
  200.4 9.0 %fusion.90 = f32[768,1536]{1,0:T(8,128)} fusion(bf16[1024,1536]{1,0:T(8,128)(2,1)} %copy-done.71, f32[1024,768]{1,0:T(8,128)} %copy-done.4, f32[768]{0:T(1024)S(1)} %copy-done.69, f32[768]{0:T(1024)S(1)} %copy-done.58, f32[1024]{0:T(1024)S(1)} %copy-done.52, f32[1024]{0:T(1024)S(1)} %copy-done.46), kind=kOutput, calls=%fused_computation.149 | convolution fusion | flops 2419851264 | bytes 11024384 | tf_op jit(solution)/shard_map/dot_general | solution.py:34
  209.4 7.6 fusion.60
  228.6 3.1 fusion.31
  231.7 77.2 %all-reduce.8 = (f32[768]{0:T(1024)S(1)}, f32[768]{0:T(1024)S(1)}, f32[2,384]{1,0:T(2,128)S(1)}, f32[768]{0:T(1024)S(1)}, f32[768]{0:T(1024)S(1)}, /*index=5*/f3...) all-reduce(f32[768]{0:T(1024)S(1)} %get-tuple-element.57, ...), channel_id=2, replica_groups=mesh['dp'=16,'mp'=2] {'dp'}, use_global_device_ids=true, to_apply=%region_19.20.clone | all-reduce | flops 6912 | bytes 55296
  313.6 4.6 fusion.42
  321.5 38.5 %reduce-scatter.8.cloned.1.call-done = f32[384,48]{0,1:T(8,128)} async-done(((f32[384,768]{0,1:T(8,128)}), f32[384,48]{0,1:T(8,128)}) %reduce-scatter.8.cloned.1.call-update) | async-done | bytes 73744 | tf_op jit(solution)/shard_map/reduce_scatter | solution.py:244
  360.1 143.2 %reduce-scatter.10.cloned.1.call-done = f32[48,1536]{1,0:T(8,128)} async-done(((f32[768,1536]{1,0:T(8,128)}), f32[48,1536]{1,0:T(8,128)}) %reduce-scatter.10.cloned.1.call-update) | async-done | bytes 294928 | tf_op jit(solution)/shard_map/reduce_scatter | solution.py:248
  503.3 143.0 %reduce-scatter.12.cloned.1.call-done = f32[1536,48]{0,1:T(8,128)} async-done(((f32[1536,768]{0,1:T(8,128)}), f32[1536,48]{0,1:T(8,128)}) %reduce-scatter.12.cloned.1.call-update) | async-done | bytes 294928 | tf_op jit(solution)/shard_map/reduce_scatter | solution.py:250
  646.2 139.2 %reduce-scatter.6.cloned.1.call-done = f32[3,48,384]{2,1,0:T(8,128)} async-done(((f32[3,768,384]{2,1,0:T(8,128)}), f32[3,48,384]{2,1,0:T(8,128)}) %reduce-scatter.6.cloned.1.call-update) | async-done | bytes 221200 | tf_op jit(solution)/shard_map/reduce_scatter | solution.py:242
  (224 shorter events, 53.9 us)
Async XLA Ops:
  7.2 65.4 %copy-start = (bf16[768,1536]{1,0:T(8,128)(2,1)S(1)}, bf16[768,1536]{1,0:T(8,128)(2,1)}, u32[]{:S(2)}) copy-start(bf16[768,1536]{1,0:T(8,128)(2,1)} %param.26) | copy-start | bytes 7077892
  7.2 62.0 %all-reduce.14.cloned.1.call-start = ((), (), s32[]{:S(2)}) async-start(), calls=%async_computation.4 | async-start | bytes 6291456 | tf_op jit(solution)/shard_map/psum | solution.py:172
  8.1 31.2 %copy-start.32 = (f32[1,1024]{1,0:T(1,128)}, f32[1,1024]{1,0:T(1,128)S(1)}, u32[]{:S(2)}) copy-start(f32[1,1024]{1,0:T(1,128)S(1)} %compare_convert_fusion) | copy-start | bytes 12292
  16.1 17.5 %copy-start.15 = (bf16[1024,384]{0,1:T(8,128)(2,1)}, bf16[1024,384]{0,1:T(8,128)(2,1)S(1)}, u32[]{:S(2)}) copy-start(bf16[1024,384]{0,1:T(8,128)(2,1)S(1)} %add_convert_fusion.5) | copy-start | bytes 2359300
  28.4 11.0 %copy-start.18 = (f32[6,64,512]{2,1,0:T(8,128)}, f32[6,64,512]{2,1,0:T(8,128)S(1)}, u32[]{:S(2)}) copy-start(f32[6,64,512]{2,1,0:T(8,128)S(1)} %fusion.17) | copy-start | bytes 2359300
  43.0 83.5 %all-reduce.16.cloned.1.call-start = ((), (), s32[]{:S(2)}) async-start(), calls=%async_computation.5 | async-start | bytes 6291456 | tf_op jit(solution)/shard_map/psum | solution.py:189
  72.1 18.0 %copy-start.4 = (f32[1024,768]{1,0:T(8,128)}, f32[1024,768]{1,0:T(8,128)S(1)}, u32[]{:S(2)}) copy-start(f32[1024,768]{1,0:T(8,128)S(1)} %get-tuple-element.90) | copy-start | bytes 9437188
  72.1 17.9 %copy-start.44 = (f32[1024]{0:T(1024)}, f32[1024]{0:T(1024)S(1)}, u32[]{:S(2)}) copy-start(f32[1024]{0:T(1024)S(1)} %broadcast_multiply_fusion.4) | copy-start | bytes 12292
  72.9 17.2 %copy-start.50 = (f32[1024]{0:T(1024)}, f32[1024]{0:T(1024)S(1)}, u32[]{:S(2)}) copy-start(f32[1024]{0:T(1024)S(1)} %add_rsqrt_fusion) | copy-start | bytes 12292
  72.9 17.2 %copy-start.27 = (bf16[1,1024,768]{2,1,0:T(8,128)(2,1)S(1)}, bf16[1,1024,768]{2,1,0:T(8,128)(2,1)}, u32[]{:S(2)}) copy-start(bf16[1,1024,768]{2,1,0:T(8,128)(2,1)} %param.17) | copy-start | bytes 4718596
  72.9 17.2 %copy-start.33 = (f32[1,1024]{1,0:T(1,128)S(1)}, f32[1,1024]{1,0:T(1,128)}, u32[]{:S(2)}) copy-start(f32[1,1024]{1,0:T(1,128)} %copy-done.32) | copy-start | bytes 12292
  72.9 17.2 %copy-start.66 = (bf16[1536,768]{1,0:T(8,128)(2,1)S(1)}, bf16[1536,768]{1,0:T(8,128)(2,1)}, u32[]{:S(2)}) copy-start(bf16[1536,768]{1,0:T(8,128)(2,1)} %param.28) | copy-start | bytes 7077892
  101.9 126.7 %all-reduce.18.cloned.1.call-start = ((), (), s32[]{:S(2)}) async-start(), calls=%async_computation.10 | async-start | bytes 12582912 | tf_op jit(solution)/shard_map/psum | solution.py:179
  103.2 23.3 %copy-start.45 = (f32[1024]{0:T(1024)S(1)}, f32[1024]{0:T(1024)}, u32[]{:S(2)}) copy-start(f32[1024]{0:T(1024)} %copy-done.44) | copy-start | bytes 12292
  103.2 23.3 %copy-start.51 = (f32[1024]{0:T(1024)S(1)}, f32[1024]{0:T(1024)}, u32[]{:S(2)}) copy-start(f32[1024]{0:T(1024)} %copy-done.50) | copy-start | bytes 12292
  103.2 23.3 %copy-start.57 = (f32[768]{0:T(1024)S(1)}, f32[768]{0:T(1024)}, u32[]{:S(2)}) copy-start(f32[768]{0:T(1024)} %param.24) | copy-start | bytes 9220
  110.3 20.8 %copy-start.28 = (bf16[1,1024,768]{2,1,0:T(8,128)(2,1)S(1)}, bf16[1,1024,768]{2,1,0:T(8,128)(2,1)}, u32[]{:S(2)}) copy-start(bf16[1,1024,768]{2,1,0:T(8,128)(2,1)} %param.17) | copy-start | bytes 4718596
  126.5 12.3 %slice-start = ((s8[12582912]{0:T(1024)(128)(4,1)}), s8[4194304]{0:T(1024)(128)(4,1)S(1)}, s32[]{:S(2)}) async-start(s8[12582912]{0:T(1024)(128)(4,1)} %bitcast.152), calls=%async_computation.11 | async-start | bytes 8388608
  131.0 7.7 slice-start.1
  131.1 7.7 slice-start.2
  145.0 19.0 %slice-start.3 = ((s8[12582912]{0:T(1024)(128)(4,1)}), s8[4194304]{0:T(1024)(128)(4,1)S(1)}, s32[]{:S(2)}) async-start(s8[12582912]{0:T(1024)(128)(4,1)} %bitcast.154), calls=%async_computation.14 | async-start | bytes 8388608
  145.0 19.0 %slice-start.4 = ((s8[12582912]{0:T(1024)(128)(4,1)}), s8[4194304]{0:T(1024)(128)(4,1)S(1)}, s32[]{:S(2)}) async-start(s8[12582912]{0:T(1024)(128)(4,1)} %bitcast.154), calls=%async_computation.15 | async-start | bytes 8388608
  155.0 9.0 %slice-start.5 = ((s8[12582912]{0:T(1024)(128)(4,1)}), s8[4194304]{0:T(1024)(128)(4,1)S(1)}, s32[]{:S(2)}) async-start(s8[12582912]{0:T(1024)(128)(4,1)} %bitcast.154), calls=%async_computation.16 | async-start | bytes 8388608
  195.0 165.1 %reduce-scatter.8.cloned.1.call-start = ((), (), s32[]{:S(2)}) async-start(), calls=%async_computation.7 | async-start | bytes 1253376 | tf_op jit(solution)/shard_map/reduce_scatter | solution.py:244
  200.3 303.0 %reduce-scatter.10.cloned.1.call-start = ((), (), s32[]{:S(2)}) async-start(), calls=%async_computation.8 | async-start | bytes 5013504 | tf_op jit(solution)/shard_map/reduce_scatter | solution.py:248
  209.4 436.8 %reduce-scatter.12.cloned.1.call-start = ((), (), s32[]{:S(2)}) async-start(), calls=%async_computation.9 | async-start | bytes 5013504 | tf_op jit(solution)/shard_map/reduce_scatter | solution.py:250
  217.0 568.4 %reduce-scatter.6.cloned.1.call-start = ((), (), s32[]{:S(2)}) async-start(), calls=%async_computation.6 | async-start | bytes 3760128 | tf_op jit(solution)/shard_map/reduce_scatter | solution.py:242
  225.1 6.6 copy-start.53
  225.1 6.6 copy-start.54
  225.1 6.6 copy-start.59
  225.1 88.5 %copy-start.62 = (f32[768]{0:T(1024)S(1)}, f32[768]{0:T(1024)}, u32[]{:S(2)}) copy-start(f32[768]{0:T(1024)} %param.29) | copy-start | bytes 9220
  313.6 471.8 %copy-start.1 = (bf16[768,1536]{1,0:T(8,128)(2,1)S(1)}, bf16[768,1536]{1,0:T(8,128)(2,1)}, u32[]{:S(2)}) copy-start(bf16[768,1536]{1,0:T(8,128)(2,1)} %param.26) | copy-start | bytes 7077892
  (53 other events, 170.4 us)
Sparse Core Ops, SparseCore 0:
  43.1 26.0 all-reduce.13
  102.0 24.4 all-reduce.15
  195.1 33.4 all-reduce.17
  233.7 126.2 reduce-scatter.7
  365.6 137.5 reduce-scatter.9
  508.8 137.3 reduce-scatter.11
  651.9 133.4 reduce-scatter.5
where the time goes:
time: 796 us; the launch traced here: 792 us
  waiting for transfers between devices  506 us (64%)
  matrix products  117 us (15%)
  blocking collectives  77.2 us (10%)
  other arithmetic  53.9 us (7%)
  local copies, waits for them, and re-layouts  19.7 us (2%)
  between operations  17.3 us (2%)
    reduce_scatter x1, waiting for transfers between devices, shards(): lax.psum_scatter(fc1_grad, 'dp', scatter_dimension=0, tiled=True)  143 us
    reduce_scatter x1, waiting for transfers between devices, shards(): lax.psum_scatter(fc2_grad, 'dp', scatter_dimension=1, tiled=True)  143 us
    reduce_scatter x1, waiting for transfers between devices, shards(): lax.psum_scatter(qkv_grad, 'dp', scatter_dimension=1, tiled=True)  139 us
    unnamed x1, blocking collectives  77.2 us
    reduce_scatter x1, waiting for transfers between devices, shards(): lax.psum_scatter(proj_grad, 'dp', scatter_dimension=1, tiled=True)  38.5 us
    dot_general x6, matrix products, product(): return jnp.dot(left_side, right_side, preferred_element_type=jnp.float32)  29.4 us
    psum x1, waiting for transfers between devices, shards(): branch = lax.psum(product(attended, proj_weight), 'mp') + proj_bias  26.1 us
    dot_general x6, matrix products, row_contract(): lax.dot_general(left_side, right_side, (((0,), (0,)), ((), ())), preferre...  25.8 us
  transfers between devices with their start and end apart: 7, of which 6 were waited for; matrix products, arithmetic and copies ran while one was open for 6% of the time, Pallas kernels for 0%

commit v1 on v0

--- a/solution.py
+++ b/solution.py
@@ -186,7 +186,11 @@
     grad_hidden = gelu_pull(grad_active)[0].astype(jnp.bfloat16)
     fc1_grad = row_contract(norm2_low, grad_hidden)
     fc1_bias_grad = jnp.sum(grad_hidden, axis=0, dtype=jnp.float32)
-    grad_norm2 = lax.psum(back_product(grad_hidden, fc1_weight), "mp")
+
+    def page_pass(x_in):
+        return jnp.sum(lax.all_gather(x_in, "mp"), axis=0)
+
+    grad_norm2 = page_pass(back_product(grad_hidden, fc1_weight))
     grad_mid_norm, norm2_gain_grad, norm2_bias_grad = norm_back(
         grad_norm2, norm2_hat, norm2_inv, norm2_gain
     )

time: 796 us -> 795 us (level)
  waiting for transfers between devices: 506 us -> 497 us
  other arithmetic: 53.9 us -> 62.3 us
    psum x1 -> x0, waiting for transfers between devices: 16.2 us -> none  [shards(): grad_norm2 = lax.psum(back_product(grad_hidden, fc1_weight), 'mp')]
    all_gather x0 -> x1, waiting for transfers between devices: none -> 9.79 us  [page_pass(): return jnp.sum(lax.all_gather(x_in, 'mp'), axis=0)]
    reduce_sum x0 -> x2, other arithmetic: none -> 8.45 us  [the longest x1 5.23 us: page_pass(): return jnp.sum(lax.all_gather(x_in, 'mp'), axis=0)]
    unnamed x165 -> x163, local copies, waits for them, and re-layouts: 17.9 us -> 17.8 us
  transfers between devices with their start and end apart: 7 -> 7, of which waited for: 6 -> 6; matrix products, arithmetic and copies ran while one was open for 6% -> 7% of each run, Pallas kernels for 0% -> 0%
where the time goes in v1:
time: 795 us; the launch traced here: 791 us
  waiting for transfers between devices  497 us (63%)
  matrix products  117 us (15%)
  blocking collectives  77.2 us (10%)
  other arithmetic  62.3 us (8%)
  local copies, waits for them, and re-layouts  19.6 us (2%)
  between operations  17.2 us (2%)
    reduce_scatter x1, waiting for transfers between devices, shards(): lax.psum_scatter(fc2_grad, 'dp', scatter_dimension=1, tiled=True)  143 us
    reduce_scatter x1, waiting for transfers between devices, shards(): lax.psum_scatter(fc1_grad, 'dp', scatter_dimension=0, tiled=True)  143 us
    reduce_scatter x1, waiting for transfers between devices, shards(): lax.psum_scatter(qkv_grad, 'dp', scatter_dimension=1, tiled=True)  139 us
    unnamed x1, blocking collectives  77.2 us
    reduce_scatter x1, waiting for transfers between devices, shards(): lax.psum_scatter(proj_grad, 'dp', scatter_dimension=1, tiled=True)  35.4 us
    dot_general x6, matrix products, product(): return jnp.dot(left_side, right_side, preferred_element_type=jnp.float32)  29.4 us
    psum x1, waiting for transfers between devices, shards(): branch = lax.psum(product(attended, proj_weight), 'mp') + proj_bias  26.1 us
    dot_general x6, matrix products, row_contract(): lax.dot_general(left_side, right_side, (((0,), (0,)), ((), ())), preferre...  25.8 us
  transfers between devices with their start and end apart: 7, of which 6 were waited for; matrix products, arithmetic and copies ran while one was open for 7% of the time, Pallas kernels for 0%

profile of v1, /device:TPU:0, one launch (start us, length us, event | category | flops | bytes accessed | tf_op | source)
XLA Modules:
  0.0 791.4 jit_solution(13417159309625524121)
XLA Ops:
  20.1 2.8 fusion.1
  24.6 3.8 fusion.17
  35.5 3.8 fusion.16
  43.0 26.1 %all-reduce.13.cloned.1.call-done = f32[1024,768]{1,0:T(8,128)} async-done(((f32[1024,768]{1,0:T(8,128)}), f32[1024,768]{1,0:T(8,128)}) %all-reduce.13.cloned.1.call-update) | async-done | bytes 3145744 | tf_op jit(solution)/shard_map/psum | solution.py:172
  69.2 2.8 fusion.94
  72.8 17.2 %multiply_convert_fusion.2 = (bf16[1024,1536]{1,0:T(8,128)(2,1)}, f32[1024,1536]{1,0:T(8,128)S(1)}, f32[1024,1536]{1,0:T(8,128)S(1)}) fusion(f32[1536]{0:T(1024)S(1)} %copy-done.66, bf16[768,1536]{1,0:T(8,128)(2,1)S(1)} %copy-done, f32[1024,768]{1,0:T(8,128)S(1)} %get-tuple-element.89, f32[768]{0:T(1024)S(1)} %copy-done.67, f32[768]{0:T(1024)S(1)} %copy-done.53, ...), kind=kOutput, calls=%fused_computation.24 | convolution fusion | flops 2523660288 | bytes 21254144 | tf_op jit(solution)/shard_map/dot_general | solution.py:30
  90.1 5.6 convert_reduce_fusion
  97.4 4.3 fusion.102
  103.0 7.0 fusion.101
  110.0 9.8 %all-gather.3.cloned.1.call-done = f32[2048,768]{1,0:T(8,128)} async-done(((f32[1024,768]{1,0:T(8,128)}), f32[2048,768]{1,0:T(8,128)}) %all-gather.3.cloned.1.call-update) | async-done | bytes 6291472 | tf_op jit(solution)/shard_map/all_gather | solution.py:191
  119.8 5.2 reduce_sum.208
  125.1 4.5 multiply_reduce_fusion.2
  129.6 4.3 convert_reduce_fusion.2
  137.3 6.2 multiply_reduce_fusion.1
  143.5 10.1 %multiply_convert_fusion.1 = bf16[6,512,1024]{2,1,0:T(8,128)(2,1)} fusion(f32[6,512,1024]{2,1,0:T(8,128)} %get-tuple-element.107, f32[6,512,1024]{2,1,0:T(8,128)S(1)} %bitcast.154, f32[6,512]{1,0:T(8,128)S(1)} %get-tuple-element.106, f32[6,512]{1,0:T(8,128)S(1)} %log_add_fusion.1), kind=kLoop, calls=%fused_computation.3 | loop fusion | flops 12582912 | bytes 31481856 | tf_op jit(solution)/shard_map/while/body/eval_jaxpr/convert_element_type | solution.py:111
  153.6 5.0 fusion.58
  158.5 4.0 fusion.103
  162.6 3.3 fusion.5
  165.9 7.5 multiply_reduce_fusion
  173.4 5.0 convert_reduce_fusion.3
  178.3 6.6 multiply_convert_fusion
  194.5 4.2 fusion.80
  198.8 9.0 %fusion.90 = f32[768,1536]{1,0:T(8,128)} fusion(bf16[1024,1536]{1,0:T(8,128)(2,1)} %copy-done.70, f32[1024,768]{1,0:T(8,128)} %copy-done.4, f32[768]{0:T(1024)S(1)} %copy-done.68, f32[768]{0:T(1024)S(1)} %copy-done.55, f32[1024]{0:T(1024)S(1)} %copy-done.49, f32[1024]{0:T(1024)S(1)} %copy-done.40), kind=kOutput, calls=%fused_computation.149 | convolution fusion | flops 2419851264 | bytes 11024384 | tf_op jit(solution)/shard_map/dot_general | solution.py:34
  207.8 7.6 fusion.60
  226.9 3.2 reduce_sum.221
  230.2 3.1 fusion.31
  233.3 77.2 %all-reduce.8 = (f32[768]{0:T(1024)S(1)}, f32[768]{0:T(1024)S(1)}, f32[2,384]{1,0:T(2,128)S(1)}, f32[768]{0:T(1024)S(1)}, f32[768]{0:T(1024)S(1)}, /*index=5*/f3...) all-reduce(f32[768]{0:T(1024)S(1)} %get-tuple-element.57, ...), channel_id=3, replica_groups=mesh['dp'=16,'mp'=2] {'dp'}, use_global_device_ids=true, to_apply=%region_19.20.clone | all-reduce | flops 6912 | bytes 55296
  315.3 4.6 fusion.42
  323.1 35.4 %reduce-scatter.8.cloned.1.call-done = f32[384,48]{0,1:T(8,128)} async-done(((f32[384,768]{0,1:T(8,128)}), f32[384,48]{0,1:T(8,128)}) %reduce-scatter.8.cloned.1.call-update) | async-done | bytes 73744 | tf_op jit(solution)/shard_map/reduce_scatter | solution.py:248
  358.5 143.2 %reduce-scatter.10.cloned.1.call-done = f32[48,1536]{1,0:T(8,128)} async-done(((f32[768,1536]{1,0:T(8,128)}), f32[48,1536]{1,0:T(8,128)}) %reduce-scatter.10.cloned.1.call-update) | async-done | bytes 294928 | tf_op jit(solution)/shard_map/reduce_scatter | solution.py:252
  501.7 143.3 %reduce-scatter.12.cloned.1.call-done = f32[1536,48]{0,1:T(8,128)} async-done(((f32[1536,768]{0,1:T(8,128)}), f32[1536,48]{0,1:T(8,128)}) %reduce-scatter.12.cloned.1.call-update) | async-done | bytes 294928 | tf_op jit(solution)/shard_map/reduce_scatter | solution.py:254
  645.0 139.3 %reduce-scatter.6.cloned.1.call-done = f32[3,48,384]{2,1,0:T(8,128)} async-done(((f32[3,768,384]{2,1,0:T(8,128)}), f32[3,48,384]{2,1,0:T(8,128)}) %reduce-scatter.6.cloned.1.call-update) | async-done | bytes 221200 | tf_op jit(solution)/shard_map/reduce_scatter | solution.py:246
  (224 shorter events, 59.2 us)
Async XLA Ops:
  7.2 65.4 %copy-start = (bf16[768,1536]{1,0:T(8,128)(2,1)S(1)}, bf16[768,1536]{1,0:T(8,128)(2,1)}, u32[]{:S(2)}) copy-start(bf16[768,1536]{1,0:T(8,128)(2,1)} %param.26) | copy-start | bytes 7077892
  7.2 5.6 copy-start.64
  7.2 5.6 copy-start.51
  7.2 5.6 copy-start.62
  7.2 61.9 %all-reduce.13.cloned.1.call-start = ((), (), s32[]{:S(2)}) async-start(), calls=%async_computation.4 | async-start | bytes 6291456 | tf_op jit(solution)/shard_map/psum | solution.py:172
  7.3 5.6 copy-start.5
  8.1 31.2 %copy-start.32 = (f32[1,1024]{1,0:T(1,128)}, f32[1,1024]{1,0:T(1,128)S(1)}, u32[]{:S(2)}) copy-start(f32[1,1024]{1,0:T(1,128)S(1)} %compare_convert_fusion) | copy-start | bytes 12292
  16.1 17.5 %copy-start.15 = (bf16[1024,384]{0,1:T(8,128)(2,1)}, bf16[1024,384]{0,1:T(8,128)(2,1)S(1)}, u32[]{:S(2)}) copy-start(bf16[1024,384]{0,1:T(8,128)(2,1)S(1)} %add_convert_fusion.5) | copy-start | bytes 2359300
  22.9 5.5 copy-start.41
  28.4 11.0 %copy-start.18 = (f32[6,64,512]{2,1,0:T(8,128)}, f32[6,64,512]{2,1,0:T(8,128)S(1)}, u32[]{:S(2)}) copy-start(f32[6,64,512]{2,1,0:T(8,128)S(1)} %fusion.17) | copy-start | bytes 2359300
  43.0 76.8 %all-gather.3.cloned.1.call-start = ((), (), s32[]{:S(2)}) async-start(), calls=%async_computation.9 | async-start | bytes 9437184 | tf_op jit(solution)/shard_map/all_gather | solution.py:191
  72.0 18.0 %copy-start.4 = (f32[1024,768]{1,0:T(8,128)}, f32[1024,768]{1,0:T(8,128)S(1)}, u32[]{:S(2)}) copy-start(f32[1024,768]{1,0:T(8,128)S(1)} %get-tuple-element.89) | copy-start | bytes 9437188
  72.1 18.0 %copy-start.38 = (f32[1024]{0:T(1024)}, f32[1024]{0:T(1024)S(1)}, u32[]{:S(2)}) copy-start(f32[1024]{0:T(1024)S(1)} %broadcast_multiply_fusion.4) | copy-start | bytes 12292
  72.8 17.2 %copy-start.47 = (f32[1024]{0:T(1024)}, f32[1024]{0:T(1024)S(1)}, u32[]{:S(2)}) copy-start(f32[1024]{0:T(1024)S(1)} %add_rsqrt_fusion) | copy-start | bytes 12292
  72.8 17.2 %copy-start.27 = (bf16[1,1024,768]{2,1,0:T(8,128)(2,1)S(1)}, bf16[1,1024,768]{2,1,0:T(8,128)(2,1)}, u32[]{:S(2)}) copy-start(bf16[1,1024,768]{2,1,0:T(8,128)(2,1)} %param.17) | copy-start | bytes 4718596
  72.8 17.2 %copy-start.33 = (f32[1,1024]{1,0:T(1,128)S(1)}, f32[1,1024]{1,0:T(1,128)}, u32[]{:S(2)}) copy-start(f32[1,1024]{1,0:T(1,128)} %copy-done.32) | copy-start | bytes 12292
  72.8 17.2 %copy-start.65 = (bf16[1536,768]{1,0:T(8,128)(2,1)S(1)}, bf16[1536,768]{1,0:T(8,128)(2,1)}, u32[]{:S(2)}) copy-start(bf16[1536,768]{1,0:T(8,128)(2,1)} %param.28) | copy-start | bytes 7077892
  101.7 128.5 %all-reduce.15.cloned.1.call-start = ((), (), s32[]{:S(2)}) async-start(), calls=%async_computation.10 | async-start | bytes 12582912 | tf_op jit(solution)/shard_map/psum | solution.py:179
  125.1 12.2 %slice-start = ((s8[12582912]{0:T(1024)(128)(4,1)}), s8[4194304]{0:T(1024)(128)(4,1)S(1)}, s32[]{:S(2)}) async-start(s8[12582912]{0:T(1024)(128)(4,1)} %bitcast.153), calls=%async_computation.11 | async-start | bytes 8388608
  129.6 6.0 copy-start.22
  129.6 7.7 slice-start.1
  129.6 7.7 slice-start.2
  143.5 19.1 %slice-start.3 = ((s8[12582912]{0:T(1024)(128)(4,1)}), s8[4194304]{0:T(1024)(128)(4,1)S(1)}, s32[]{:S(2)}) async-start(s8[12582912]{0:T(1024)(128)(4,1)} %bitcast.155), calls=%async_computation.14 | async-start | bytes 8388608
  143.5 19.1 %slice-start.4 = ((s8[12582912]{0:T(1024)(128)(4,1)}), s8[4194304]{0:T(1024)(128)(4,1)S(1)}, s32[]{:S(2)}) async-start(s8[12582912]{0:T(1024)(128)(4,1)} %bitcast.155), calls=%async_computation.15 | async-start | bytes 8388608
  153.5 9.0 %slice-start.5 = ((s8[12582912]{0:T(1024)(128)(4,1)}), s8[4194304]{0:T(1024)(128)(4,1)S(1)}, s32[]{:S(2)}) async-start(s8[12582912]{0:T(1024)(128)(4,1)} %bitcast.155), calls=%async_computation.16 | async-start | bytes 8388608
  193.4 165.1 %reduce-scatter.8.cloned.1.call-start = ((), (), s32[]{:S(2)}) async-start(), calls=%async_computation.6 | async-start | bytes 1253376 | tf_op jit(solution)/shard_map/reduce_scatter | solution.py:248
  198.7 303.0 %reduce-scatter.10.cloned.1.call-start = ((), (), s32[]{:S(2)}) async-start(), calls=%async_computation.7 | async-start | bytes 5013504 | tf_op jit(solution)/shard_map/reduce_scatter | solution.py:252
  207.8 437.2 %reduce-scatter.12.cloned.1.call-start = ((), (), s32[]{:S(2)}) async-start(), calls=%async_computation.8 | async-start | bytes 5013504 | tf_op jit(solution)/shard_map/reduce_scatter | solution.py:254
  215.4 568.9 %reduce-scatter.6.cloned.1.call-start = ((), (), s32[]{:S(2)}) async-start(), calls=%async_computation.5 | async-start | bytes 3760128 | tf_op jit(solution)/shard_map/reduce_scatter | solution.py:246
  230.2 85.0 %copy-start.61 = (f32[768]{0:T(1024)S(1)}, f32[768]{0:T(1024)}, u32[]{:S(2)}) copy-start(f32[768]{0:T(1024)} %param.29) | copy-start | bytes 9220
  315.2 5.8 copy-start.10
  315.2 469.1 %copy-start.1 = (bf16[768,1536]{1,0:T(8,128)(2,1)S(1)}, bf16[768,1536]{1,0:T(8,128)(2,1)}, u32[]{:S(2)}) copy-start(bf16[768,1536]{1,0:T(8,128)(2,1)} %param.26) | copy-start | bytes 7077892
  (52 other events, 150.0 us)
Sparse Core Ops, SparseCore 0:
  43.1 26.0 all-reduce.12
  101.8 17.9 all-gather.2
  193.5 33.4 all-reduce.14
  232.1 126.3 reduce-scatter.7
  364.1 137.5 reduce-scatter.9
  507.3 137.7 reduce-scatter.11
  650.7 133.5 reduce-scatter.5
